TPU v7x, 128 devices: a whole 4x4x4 slice. The times are simulated.
128 devices in a mesh: ex: 16 (over z, y), feat: 8 (over x, core).
Axes of the slice: x: 4, y: 4, z: 4, core: 2. Of those that a mesh axis runs over, the one named last changes fastest.
Arguments:
- tiles: bfloat16 [16, 8, 384, 128, 128], P('ex', 'feat'), may hold values from -0.5 to 0.5
- row_index: int32 [16, 8, 384], P('ex', 'feat'), may hold values from 0 to 2047
- col_index: int32 [16, 8, 384], P('ex', 'feat'), may hold values from 0 to 4095
- weights: bfloat16 [32768, 128], P('feat'), may hold values from -6 to 6
- val_grad: float32 [32768, 128], P('feat'), may hold values from -6 to 6
- field_map: int32 [32768, 128], P('feat'), may hold values from 0 to 63
- field_lambda: float32 [64], replicated, may hold values from 0.05 to 2
Outputs:
- solution: float32 [32768, 128], P(('feat', 'ex'))
- hypergrad: float32 [64], replicated
Inputs may be any that keep to these rules, and one draw needn't show every extreme that they name: `row_index`: local row tile of a stored tile within its device's 2048 row tiles. `col_index`: local column tile of a stored tile within its device's 4096 column tiles.
All inputs are finite; a program needn't handle non-finite values.
Results may differ from a plain program's by a relative error of at most 0.0021.
Values may be sent and summed in bfloat16 or wider, within the bound.
A program may use at most 128 MiB of HBM per device.

v0:
```python
import math
import jax
import jax.numpy as jnp
from jax import lax
from jax.sharding import PartitionSpec as P

RT_DEV = 2048
ITERS = 3


def on_device(tiles, row_index, col_index, weights, val_grad, field_map, field_lambda):
    tile_count = tiles.shape[2]
    tile_width = tiles.shape[3]
    tile_stack = tiles.reshape(tile_count, tile_width, tile_width)
    row_ids = row_index.reshape(tile_count)
    col_ids = col_index.reshape(tile_count)
    segment = weights.shape[0]
    share_len = segment // lax.axis_size("ex")
    offset = lax.axis_index("ex") * share_len
    field_count = field_lambda.shape[0]
    labels = jnp.arange(field_count, dtype=jnp.int32)
    norm_scale = 1.0 / math.sqrt(segment * tile_width * lax.axis_size("feat") // field_count)

    def own_part(vector):
        return lax.dynamic_slice_in_dim(vector, offset, share_len, 0)

    def forward(vec_b):
        pieces = jnp.take(vec_b, col_ids, axis=0)
        products = jnp.einsum("tij,tj->ti", tile_stack, pieces, preferred_element_type=jnp.float32)
        partial_rows = jnp.zeros((RT_DEV, tile_width), jnp.float32).at[row_ids].add(products)
        return lax.psum(partial_rows, "feat")

    def lookup(field_block):
        matches = field_block[..., None] == labels
        return jnp.sum(jnp.where(matches, field_lambda, 0.0), axis=-1)

    margin = forward(weights)
    prob = jax.nn.sigmoid(margin)
    curv_weight = prob * (1.0 - prob)
    count = field_map.shape[0]
    block_rows = math.gcd(count, 256)
    lam_part = lax.map(lookup, field_map.reshape(-1, block_rows, tile_width)).reshape(
        count, tile_width
    )
    residual = val_grad

    def local(vector):
        return own_part(vector)

    direction = residual
    solution = jnp.zeros_like(residual)
    dir_b = val_grad.astype(jnp.bfloat16)
    mine = local(residual)
    norm_now = lax.psum(jnp.sum(mine * mine), ("ex", "feat"))
    for step in range(ITERS):
        rows_sum = forward(dir_b)
        scaled_part = (curv_weight * rows_sum).astype(jnp.bfloat16)
        backward_pieces = jnp.take(scaled_part, row_ids, axis=0)
        backward_products = jnp.einsum(
            "tij,ti->tj", tile_stack, backward_pieces, preferred_element_type=jnp.float32
        )
        partial_feat = (
            jnp.zeros((segment, tile_width), jnp.float32).at[col_ids].add(backward_products)
        )
        image = lax.psum(partial_feat, "ex") + lam_part * direction
        own_dir = local(direction)
        own_image = local(image)
        curv_sum = lax.psum(jnp.sum(own_dir * own_image), ("ex", "feat"))
        step_size = norm_now / curv_sum
        solution = solution + step_size * direction
        residual = residual - step_size * image
        if step + 1 < ITERS:
            own_res = local(residual)
            next_norm = lax.psum(jnp.sum(own_res * own_res), ("ex", "feat"))
        if step + 1 < ITERS:
            direction = residual + next_norm / norm_now * direction
            norm_now = next_norm
            dir_b = direction.astype(jnp.bfloat16)
    own_solution = local(solution)
    own_terms = own_solution * own_part(weights).astype(jnp.float32)
    own_fields = own_part(field_map)
    share_block = math.gcd(share_len, 256)

    def field_sums(element):
        term_block, field_block = element
        matches = field_block[..., None] == labels
        return jnp.sum(jnp.where(matches, term_block[..., None], 0.0), axis=(0, 1))

    per_block = lax.map(
        field_sums,
        (
            own_terms.reshape(-1, share_block, tile_width),
            own_fields.reshape(-1, share_block, tile_width),
        ),
    )
    totals = lax.psum(jnp.sum(per_block, axis=0), ("ex", "feat"))
    hypergrad = -field_lambda * totals * norm_scale
    return (own_solution, hypergrad)


def solution(mesh):
    return jax.shard_map(
        on_device,
        mesh=mesh,
        in_specs=(
            P("ex", "feat", None, None, None),
            P("ex", "feat", None),
            P("ex", "feat", None),
            P("feat", None),
            P("feat", None),
            P("feat", None),
            P(),
        ),
        out_specs=(P(("feat", "ex"), None), P()),
        check_vma=False,
    )
```

profile of v0, /device:TPU:1, one launch (start us, length us, event | category | flops | bytes accessed | tf_op | source)
XLA Modules:
  0.0 994.2 jit_solution(16957785030988315214)
XLA Ops:
  12.9 10.9 %fusion.14 = f32[384,1,128]{2,1,0:T(1,128)S(1)} fusion(bf16[1,1,384,128,128]{4,3,2,1,0:T(8,128)(2,1)} %param.13, bf16[384,128,1]{1,0,2:T(8,128)(2,1)S(1)} %get-tuple-element.77), kind=kOutput, calls=%fused_computation.31 | convolution fusion | flops 12582912 | bytes 12877824 | tf_op jit(solution)/shard_map/tij,tj->ti/dot_general | solution.py:29
  23.8 6.6 fusion.12
  36.7 66.6 %all-reduce.19.cloned.1.call-done = (f32[2048,128]{1,0:T(8,128)}, f32[2048,128]{1,0:T(8,128)}) async-done(((f32[2048,128]{1,0:T(8,128)}, f32[2048,128]{1,0:T(8,128)}), (f32[2048,128]{1,0:T(8,128)}, f32[2048,128]{1,0:T(8,128)})) %all-reduce.19.cloned.1.call-update) | async-done | bytes 2097168 | tf_op jit(solution)/shard_map/psum | solution.py:31
  106.7 6.4 fusion.10
  116.4 71.8 %while.3 = (s32[]{:T(128)}, f32[16,256,128]{2,1,0:T(8,128)}, s32[16,256,128]{2,1,0:T(8,128)}, f32[64]{0:T(128)S(1)}, s32[]{:T(128)}) while((s32[]{:T(128)}, f32[16,256,128]{2,1,0:T(8,128)}, s32[16,256,128]{2,1,0:T(8,128)}, f32[64]{0:T(128)S(1)}, s32[]{:T(128)}) %tuple.52), condition=%wide.region_10.13_spmd.clone, body=%wide.region_8.12_spmd.clone.sunk | while | flops 6258690 | bytes 787265 | solution.py:42
  188.2 19.2 %all-reduce.9.cloned.1.call-done = f32[4096,128]{1,0:T(8,128)} async-done(((f32[4096,128]{1,0:T(8,128)}), f32[4096,128]{1,0:T(8,128)}) %all-reduce.9.cloned.1.call-update) | async-done | bytes 2097168 | tf_op jit(solution)/shard_map/psum | solution.py:65
  207.4 3.9 multiply_add_fusion.3
  212.8 65.3 %all-reduce = (f32[]{:T(128)}, f32[]{:T(128)}) all-reduce(f32[]{:T(128)} %get-tuple-element.58, f32[]{:T(128)} %get-tuple-element.57), channel_id=1, replica_groups=mesh['ex'=16,'feat'=8] {'ex','feat'}, use_global_device_ids=true, to_apply=%region_1.2 | all-reduce | flops 2 | bytes 16 | tf_op jit(solution)/shard_map/psum | solution.py:54
  284.2 62.7 %psum.103 = f32[]{:T(128)} all-reduce(f32[]{:T(128)} %multiply_reduce_fusion.2), channel_id=1, replica_groups=mesh['ex'=16,'feat'=8] {'ex','feat'}, use_global_device_ids=true, to_apply=%region_14.17 | all-reduce | flops 1 | bytes 8 | tf_op jit(solution)/shard_map/psum | solution.py:74
  353.0 9.5 fusion.8
  365.4 57.4 %all-reduce.11.cloned.1.call-done = f32[2048,128]{1,0:T(8,128)} async-done(((f32[2048,128]{1,0:T(8,128)}), f32[2048,128]{1,0:T(8,128)}) %all-reduce.11.cloned.1.call-update) | async-done | bytes 1048592 | tf_op jit(solution)/shard_map/psum | solution.py:31
  427.6 6.4 fusion.6
  434.0 3.3 scatter_custom_fusion.4
  437.4 90.8 %all-reduce.13.cloned.1.call-done = f32[4096,128]{1,0:T(8,128)} async-done(((f32[4096,128]{1,0:T(8,128)}), f32[4096,128]{1,0:T(8,128)}) %all-reduce.13.cloned.1.call-update) | async-done | bytes 2097168 | tf_op jit(solution)/shard_map/psum | solution.py:65
  534.1 65.4 %psum.106 = f32[]{:T(128)} all-reduce(f32[]{:T(128)} %multiply_reduce_fusion.1), channel_id=1, replica_groups=mesh['ex'=16,'feat'=8] {'ex','feat'}, use_global_device_ids=true, to_apply=%region_20.23 | all-reduce | flops 1 | bytes 8 | tf_op jit(solution)/shard_map/psum | solution.py:68
  605.2 62.8 %psum.107 = f32[]{:T(128)} all-reduce(f32[]{:T(128)} %multiply_reduce_fusion), channel_id=1, replica_groups=mesh['ex'=16,'feat'=8] {'ex','feat'}, use_global_device_ids=true, to_apply=%region_22.25 | all-reduce | flops 1 | bytes 8 | tf_op jit(solution)/shard_map/psum | solution.py:74
  669.3 4.3 fusion.41
  676.3 9.5 fusion.4
  688.6 57.5 %all-reduce.15.cloned.1.call-done = f32[2048,128]{1,0:T(8,128)} async-done(((f32[2048,128]{1,0:T(8,128)}), f32[2048,128]{1,0:T(8,128)}) %all-reduce.15.cloned.1.call-update) | async-done | bytes 1048592 | tf_op jit(solution)/shard_map/psum | solution.py:31
  750.9 6.4 fusion.2
  757.3 3.3 scatter_custom_fusion.6
  760.6 90.9 %all-reduce.17.cloned.1.call-done = f32[4096,128]{1,0:T(8,128)} async-done(((f32[4096,128]{1,0:T(8,128)}), f32[4096,128]{1,0:T(8,128)}) %all-reduce.17.cloned.1.call-update) | async-done | bytes 2097168 | tf_op jit(solution)/shard_map/psum | solution.py:65
  854.1 65.4 %psum.110 = f32[]{:T(128)} all-reduce(f32[]{:T(128)} %fusion.38), channel_id=1, replica_groups=mesh['ex'=16,'feat'=8] {'ex','feat'}, use_global_device_ids=true, to_apply=%region_28.31 | all-reduce | flops 1 | bytes 8 | tf_op jit(solution)/shard_map/psum | solution.py:68
  924.1 62.6 %psum.111 = f32[64]{0:T(128)S(1)} all-reduce(f32[64]{0:T(128)S(1)} %select_reduce_fusion.1), channel_id=1, replica_groups=mesh['ex'=16,'feat'=8] {'ex','feat'}, use_global_device_ids=true, to_apply=%region_30.33 | all-reduce | flops 64 | bytes 512 | tf_op jit(solution)/shard_map/psum | solution.py:96
  (123 shorter events, 136.1 us)
Async XLA Ops:
  7.2 4.1 copy-start.5
  7.2 96.1 %all-reduce.19.cloned.1.call-start = ((), (), s32[]{:S(2)}) async-start(), calls=%async_computation.5 | async-start | bytes 4194304 | tf_op jit(solution)/shard_map/psum | solution.py:31
  8.0 4.7 copy-start.7
  8.0 4.7 copy-start.8
  12.9 10.9 %copy-start = (bf16[1,1,384,128,128]{4,3,2,1,0:T(8,128)(2,1)S(1)}, bf16[1,1,384,128,128]{4,3,2,1,0:T(8,128)(2,1)}, u32[]{:S(2)}) copy-start(bf16[1,1,384,128,128]{4,3,2,1,0:T(8,128)(2,1)} %param.13) | copy-start | bytes 37748740
  36.1 171.3 %all-reduce.9.cloned.1.call-start = ((), (), s32[]{:S(2)}) async-start(), calls=%async_computation | async-start | bytes 4194304 | tf_op jit(solution)/shard_map/psum | solution.py:65
  113.1 3.3 copy-start.6
  116.3 91.1 %copy-start.1 = (f32[4096,128]{1,0:T(8,128)S(1)}, f32[4096,128]{1,0:T(8,128)}, u32[]{:S(2)}) copy-start(f32[4096,128]{1,0:T(8,128)} %param.17) | copy-start | bytes 6291460
  116.3 306.5 %all-reduce.11.cloned.1.call-start = ((), (), s32[]{:S(2)}) async-start(), calls=%async_computation.1 | async-start | bytes 2097152 | tf_op jit(solution)/shard_map/psum | solution.py:31
  362.5 60.4 %copy-start.2 = (f32[2048,128]{1,0:T(8,128)S(1)}, f32[2048,128]{1,0:T(8,128)}, u32[]{:S(2)}) copy-start(f32[2048,128]{1,0:T(8,128)} %get-tuple-element.70) | copy-start | bytes 3145732
  365.4 162.8 %all-reduce.13.cloned.1.call-start = ((), (), s32[]{:S(2)}) async-start(), calls=%async_computation.2 | async-start | bytes 4194304 | tf_op jit(solution)/shard_map/psum | solution.py:65
  437.3 308.8 %all-reduce.15.cloned.1.call-start = ((), (), s32[]{:S(2)}) async-start(), calls=%async_computation.3 | async-start | bytes 2097152 | tf_op jit(solution)/shard_map/psum | solution.py:31
  531.3 1.3 copy-start.4
  603.3 1.3 copy-start.3
  688.6 162.9 %all-reduce.17.cloned.1.call-start = ((), (), s32[]{:S(2)}) async-start(), calls=%async_computation.4 | async-start | bytes 4194304 | tf_op jit(solution)/shard_map/psum | solution.py:65
Sparse Core Ops, SparseCore 0:
  36.2 66.9 all-reduce.18
  116.5 90.8 all-reduce.8
  365.5 57.3 all-reduce.10
  437.4 90.6 all-reduce.12
  688.7 57.3 all-reduce.14
  760.8 90.7 all-reduce.16
where the time goes:
time: 1000 us; the launch traced here: 994 us
  blocking collectives  384 us (38%)
  waiting for transfers between devices  382 us (38%)
  other arithmetic  108 us (11%)
  matrix products  55.5 us (6%)
  local copies, waits for them, and re-layouts  41.8 us (4%)
  between operations  21.3 us (2%)
    psum x3, waiting for transfers between devices, on_device(): image = lax.psum(partial_feat, 'ex') + lam_part * direction  201 us
    psum x3, waiting for transfers between devices, forward(): return lax.psum(partial_rows, 'feat')  182 us
    psum x2, blocking collectives, on_device(): curv_sum = lax.psum(jnp.sum(own_dir * own_image), ('ex', 'feat'))  131 us
    psum x2, blocking collectives, on_device(): next_norm = lax.psum(jnp.sum(own_res * own_res), ('ex', 'feat'))  125 us
    psum x1, blocking collectives, on_device(): norm_now = lax.psum(jnp.sum(mine * mine), ('ex', 'feat'))  65.3 us
    psum x1, blocking collectives, on_device(): totals = lax.psum(jnp.sum(per_block, axis=0), ('ex', 'feat'))  62.6 us
    reduce_sum x16, other arithmetic, lookup(): return jnp.sum(jnp.where(matches, field_lambda, 0.0), axis=-1)  46.3 us
    dot_general x4, matrix products, forward(): jnp.einsum('tij,tj->ti', tile_stack, pieces, preferred_element_type=jnp.f...  36.4 us
  transfers between devices with their start and end apart: 6, of which 6 were waited for; matrix products, arithmetic and copies ran while one was open for 7% of the time, Pallas kernels for 0%

commit v1 on v0

--- a/solution.py
+++ b/solution.py
@@ -93,7 +93,7 @@
             own_fields.reshape(-1, share_block, tile_width),
         ),
     )
-    totals = lax.psum(jnp.sum(per_block, axis=0), ("ex", "feat"))
+    totals = lax.psum(lax.psum(jnp.sum(per_block, axis=0), "feat"), "ex")
     hypergrad = -field_lambda * totals * norm_scale
     return (own_solution, hypergrad)
 

time: 1000 us -> 989 us (0.989)
  blocking collectives: 384 us -> 365 us
    psum x1 -> x2, blocking collectives: 62.6 us -> 43.5 us  [on_device(): totals = lax.psum(lax.psum(jnp.sum(per_block, axis=0), 'feat'), 'ex')]
where the time goes in v1:
time: 989 us; the launch traced here: 975 us
  waiting for transfers between devices  382 us (39%)
  blocking collectives  365 us (37%)
  other arithmetic  108 us (11%)
  matrix products  55.5 us (6%)
  local copies, waits for them, and re-layouts  41.8 us (4%)
  between operations  21.3 us (2%)
    psum x3, waiting for transfers between devices, on_device(): image = lax.psum(partial_feat, 'ex') + lam_part * direction  201 us
    psum x3, waiting for transfers between devices, forward(): return lax.psum(partial_rows, 'feat')  182 us
    psum x2, blocking collectives, on_device(): curv_sum = lax.psum(jnp.sum(own_dir * own_image), ('ex', 'feat'))  131 us
    psum x2, blocking collectives, on_device(): next_norm = lax.psum(jnp.sum(own_res * own_res), ('ex', 'feat'))  125 us
    psum x1, blocking collectives, on_device(): norm_now = lax.psum(jnp.sum(mine * mine), ('ex', 'feat'))  65.3 us
    reduce_sum x16, other arithmetic, lookup(): return jnp.sum(jnp.where(matches, field_lambda, 0.0), axis=-1)  46.3 us
    psum x2, blocking collectives, on_device(): totals = lax.psum(lax.psum(jnp.sum(per_block, axis=0), 'feat'), 'ex')  43.5 us
    dot_general x4, matrix products, forward(): jnp.einsum('tij,tj->ti', tile_stack, pieces, preferred_element_type=jnp.f...  36.4 us
  transfers between devices with their start and end apart: 6, of which 6 were waited for; matrix products, arithmetic and copies ran while one was open for 7% of the time, Pallas kernels for 0%

profile of v1, /device:TPU:1, one launch (start us, length us, event | category | flops | bytes accessed | tf_op | source)
XLA Modules:
  0.0 975.2 jit_solution(17446023334320487343)
XLA Ops:
  12.9 10.9 %fusion.14 = f32[384,1,128]{2,1,0:T(1,128)S(1)} fusion(bf16[1,1,384,128,128]{4,3,2,1,0:T(8,128)(2,1)} %param.13, bf16[384,128,1]{1,0,2:T(8,128)(2,1)S(1)} %get-tuple-element.77), kind=kOutput, calls=%fused_computation.31 | convolution fusion | flops 12582912 | bytes 12877824 | tf_op jit(solution)/shard_map/tij,tj->ti/dot_general | solution.py:29
  23.8 6.6 fusion.12
  36.7 66.6 %all-reduce.19.cloned.1.call-done = (f32[2048,128]{1,0:T(8,128)}, f32[2048,128]{1,0:T(8,128)}) async-done(((f32[2048,128]{1,0:T(8,128)}, f32[2048,128]{1,0:T(8,128)}), (f32[2048,128]{1,0:T(8,128)}, f32[2048,128]{1,0:T(8,128)})) %all-reduce.19.cloned.1.call-update) | async-done | bytes 2097168 | tf_op jit(solution)/shard_map/psum | solution.py:31
  106.7 6.4 fusion.10
  116.4 71.8 %while.3 = (s32[]{:T(128)}, f32[16,256,128]{2,1,0:T(8,128)}, s32[16,256,128]{2,1,0:T(8,128)}, f32[64]{0:T(128)S(1)}, s32[]{:T(128)}) while((s32[]{:T(128)}, f32[16,256,128]{2,1,0:T(8,128)}, s32[16,256,128]{2,1,0:T(8,128)}, f32[64]{0:T(128)S(1)}, s32[]{:T(128)}) %tuple.52), condition=%wide.region_10.13_spmd.clone, body=%wide.region_8.12_spmd.clone.sunk | while | flops 6258690 | bytes 787265 | solution.py:42
  188.2 19.2 %all-reduce.9.cloned.1.call-done = f32[4096,128]{1,0:T(8,128)} async-done(((f32[4096,128]{1,0:T(8,128)}), f32[4096,128]{1,0:T(8,128)}) %all-reduce.9.cloned.1.call-update) | async-done | bytes 2097168 | tf_op jit(solution)/shard_map/psum | solution.py:65
  207.4 3.9 multiply_add_fusion.3
  212.8 65.3 %all-reduce = (f32[]{:T(128)}, f32[]{:T(128)}) all-reduce(f32[]{:T(128)} %get-tuple-element.58, f32[]{:T(128)} %get-tuple-element.57), channel_id=1, replica_groups=mesh['ex'=16,'feat'=8] {'ex','feat'}, use_global_device_ids=true, to_apply=%region_1.2 | all-reduce | flops 2 | bytes 16 | tf_op jit(solution)/shard_map/psum | solution.py:54
  284.2 62.7 %psum.110 = f32[]{:T(128)} all-reduce(f32[]{:T(128)} %multiply_reduce_fusion.2), channel_id=1, replica_groups=mesh['ex'=16,'feat'=8] {'ex','feat'}, use_global_device_ids=true, to_apply=%region_14.17 | all-reduce | flops 1 | bytes 8 | tf_op jit(solution)/shard_map/psum | solution.py:74
  353.0 9.5 fusion.8
  365.4 57.4 %all-reduce.11.cloned.1.call-done = f32[2048,128]{1,0:T(8,128)} async-done(((f32[2048,128]{1,0:T(8,128)}), f32[2048,128]{1,0:T(8,128)}) %all-reduce.11.cloned.1.call-update) | async-done | bytes 1048592 | tf_op jit(solution)/shard_map/psum | solution.py:31
  427.6 6.4 fusion.6
  434.0 3.3 scatter_custom_fusion.4
  437.4 90.8 %all-reduce.13.cloned.1.call-done = f32[4096,128]{1,0:T(8,128)} async-done(((f32[4096,128]{1,0:T(8,128)}), f32[4096,128]{1,0:T(8,128)}) %all-reduce.13.cloned.1.call-update) | async-done | bytes 2097168 | tf_op jit(solution)/shard_map/psum | solution.py:65
  534.1 65.4 %psum.113 = f32[]{:T(128)} all-reduce(f32[]{:T(128)} %multiply_reduce_fusion.1), channel_id=1, replica_groups=mesh['ex'=16,'feat'=8] {'ex','feat'}, use_global_device_ids=true, to_apply=%region_20.23 | all-reduce | flops 1 | bytes 8 | tf_op jit(solution)/shard_map/psum | solution.py:68
  605.2 62.8 %psum.114 = f32[]{:T(128)} all-reduce(f32[]{:T(128)} %multiply_reduce_fusion), channel_id=1, replica_groups=mesh['ex'=16,'feat'=8] {'ex','feat'}, use_global_device_ids=true, to_apply=%region_22.25 | all-reduce | flops 1 | bytes 8 | tf_op jit(solution)/shard_map/psum | solution.py:74
  669.3 4.3 fusion.41
  676.3 9.5 fusion.4
  688.6 57.5 %all-reduce.15.cloned.1.call-done = f32[2048,128]{1,0:T(8,128)} async-done(((f32[2048,128]{1,0:T(8,128)}), f32[2048,128]{1,0:T(8,128)}) %all-reduce.15.cloned.1.call-update) | async-done | bytes 1048592 | tf_op jit(solution)/shard_map/psum | solution.py:31
  750.9 6.4 fusion.2
  760.6 90.9 %all-reduce.17.cloned.1.call-done = f32[4096,128]{1,0:T(8,128)} async-done(((f32[4096,128]{1,0:T(8,128)}), f32[4096,128]{1,0:T(8,128)}) %all-reduce.17.cloned.1.call-update) | async-done | bytes 2097168 | tf_op jit(solution)/shard_map/psum | solution.py:65
  854.1 65.4 %psum.117 = f32[]{:T(128)} all-reduce(f32[]{:T(128)} %fusion.38), channel_id=1, replica_groups=mesh['ex'=16,'feat'=8] {'ex','feat'}, use_global_device_ids=true, to_apply=%region_28.31 | all-reduce | flops 1 | bytes 8 | tf_op jit(solution)/shard_map/psum | solution.py:68
  924.1 12.9 %psum.118 = f32[64]{0:T(128)S(1)} all-reduce(f32[64]{0:T(128)S(1)} %select_reduce_fusion.1), channel_id=1, replica_groups=mesh['ex'=16,'feat'=8] {'feat'}, use_global_device_ids=true, to_apply=%region_30.33 | all-reduce | flops 64 | bytes 512 | tf_op jit(solution)/shard_map/psum | solution.py:96
  937.0 30.6 %psum.119 = f32[64]{0:T(128)S(1)} all-reduce(f32[64]{0:T(128)S(1)} %psum.118), channel_id=1, replica_groups=mesh['ex'=16,'feat'=8] {'ex'}, use_global_device_ids=true, to_apply=%region_31.34 | all-reduce | flops 64 | bytes 512 | tf_op jit(solution)/shard_map/psum | solution.py:96
  (124 shorter events, 139.4 us)
Async XLA Ops:
  7.2 4.1 copy-start.5
  7.2 96.1 %all-reduce.19.cloned.1.call-start = ((), (), s32[]{:S(2)}) async-start(), calls=%async_computation.5 | async-start | bytes 4194304 | tf_op jit(solution)/shard_map/psum | solution.py:31
  8.0 4.7 copy-start.7
  8.0 4.7 copy-start.8
  12.9 10.9 %copy-start = (bf16[1,1,384,128,128]{4,3,2,1,0:T(8,128)(2,1)S(1)}, bf16[1,1,384,128,128]{4,3,2,1,0:T(8,128)(2,1)}, u32[]{:S(2)}) copy-start(bf16[1,1,384,128,128]{4,3,2,1,0:T(8,128)(2,1)} %param.13) | copy-start | bytes 37748740
  36.1 171.3 %all-reduce.9.cloned.1.call-start = ((), (), s32[]{:S(2)}) async-start(), calls=%async_computation | async-start | bytes 4194304 | tf_op jit(solution)/shard_map/psum | solution.py:65
  113.1 3.3 copy-start.6
  116.3 91.1 %copy-start.1 = (f32[4096,128]{1,0:T(8,128)S(1)}, f32[4096,128]{1,0:T(8,128)}, u32[]{:S(2)}) copy-start(f32[4096,128]{1,0:T(8,128)} %param.17) | copy-start | bytes 6291460
  116.3 306.5 %all-reduce.11.cloned.1.call-start = ((), (), s32[]{:S(2)}) async-start(), calls=%async_computation.1 | async-start | bytes 2097152 | tf_op jit(solution)/shard_map/psum | solution.py:31
  362.5 60.4 %copy-start.2 = (f32[2048,128]{1,0:T(8,128)S(1)}, f32[2048,128]{1,0:T(8,128)}, u32[]{:S(2)}) copy-start(f32[2048,128]{1,0:T(8,128)} %get-tuple-element.70) | copy-start | bytes 3145732
  365.4 162.8 %all-reduce.13.cloned.1.call-start = ((), (), s32[]{:S(2)}) async-start(), calls=%async_computation.2 | async-start | bytes 4194304 | tf_op jit(solution)/shard_map/psum | solution.py:65
  437.3 308.8 %all-reduce.15.cloned.1.call-start = ((), (), s32[]{:S(2)}) async-start(), calls=%async_computation.3 | async-start | bytes 2097152 | tf_op jit(solution)/shard_map/psum | solution.py:31
  531.3 1.3 copy-start.4
  603.3 1.3 copy-start.3
  688.6 162.9 %all-reduce.17.cloned.1.call-start = ((), (), s32[]{:S(2)}) async-start(), calls=%async_computation.4 | async-start | bytes 4194304 | tf_op jit(solution)/shard_map/psum | solution.py:65
Sparse Core Ops, SparseCore 0:
  36.2 66.9 all-reduce.18
  116.5 90.8 all-reduce.8
  365.5 57.3 all-reduce.10
  437.4 90.6 all-reduce.12
  688.7 57.3 all-reduce.14
  760.8 90.7 all-reduce.16
